TPU v7x, 32 devices: a whole 2x2x4 slice. The times are simulated.
32 devices in a mesh: clips: 2 (over y), ha: 8 (over z, x), wa: 2 (over core).
Axes of the slice: x: 2, y: 2, z: 4, core: 2. Of those that a mesh axis runs over, the one named last changes fastest.
Arguments:
- tokens: bfloat16 [5120, 5120], P(('clips', 'ha', 'wa')), parts along dimension 0, may hold values from -640 to 640
- timestep: int32 [2], P('clips'), parts along dimension 0, may hold values from 0 to 49
- time_table: float32 [50, 5120], replicated, may hold values from -3 to 3
- modulation: float32 [2, 5120], replicated, may hold values from -3 to 3
- head_weight: bfloat16 [5120, 64], replicated, may hold values from -0.078125 to 0.078125
- head_bias: float32 [64], replicated, may hold values from -3 to 3
- latent_std: float32 [16], replicated, may hold values from 0.5 to 2
- latent_mean: float32 [16], replicated, may hold values from -3 to 3
- conv_in_weight: bfloat16 [432, 384], replicated, may hold values from -0.3125 to 0.3125
- conv_in_bias: float32 [384], replicated, may hold values from -3 to 3
- norm_gain: float32 [384], replicated, may hold values from 0.1 to 1.9
- conv_weight: bfloat16 [10368, 384], P(None, 'wa'), may hold values from -0.0625 to 0.0625
- conv_bias: float32 [384], replicated, may hold values from -3 to 3
Outputs:
- block_input: bfloat16 [8, 16, 160, 384], P('clips', 'ha', 'wa'), parts along dimension 0
- block_mid: bfloat16 [8, 16, 160, 384], P('clips', 'ha', 'wa'), parts along dimension 0
There are 2 independent parts, one for each index of `clips`. A program takes and returns all parts, laid end to end along the dimension named above; an argument that names none is the same for every part. Nothing has to cross between parts.
All inputs are finite; a program needn't handle non-finite values.
Results may differ from a plain program's by a relative error of at most 0.0058.
Values may be sent and summed in bfloat16 or wider, within the bound.
A program may use at most 128 MiB of HBM per device.

v0:
```python
import jax
import jax.numpy as jnp
from jax import lax
from jax.sharding import PartitionSpec as P

PATCH = 2
F = 4
PR = 1
PW = 40


def with_halo(x, sides, width):
    for axis, dim in sides:
        count, length = (lax.axis_size(axis), x.shape[dim])
        up = [(i, (i + 1) % count) for i in range(count - 1)]
        down = [(j, i) for i, j in up]
        last = lax.slice_in_dim(x, length - width, length, axis=dim)
        first = lax.slice_in_dim(x, 0, width, axis=dim)
        before = lax.ppermute(last, axis, up)
        after = lax.ppermute(first, axis, down)
        x = jnp.concatenate([before, x, after], axis=dim)
    return x


def head_latent(
    tokens, timestep, time_table, modulation, head_weight, head_bias, latent_std, latent_mean
):
    select = jnp.arange(time_table.shape[0], dtype=jnp.int32) == timestep[0]
    embed = jnp.sum(jnp.where(select[:, None], time_table, jnp.zeros_like(time_table)), axis=0)
    shift_row = modulation[0] + embed
    scale_row = modulation[1] + embed
    values = tokens.astype(jnp.float32)
    centre = jnp.mean(values, axis=-1, keepdims=True)
    spread = jnp.mean(jnp.square(values - centre), axis=-1, keepdims=True)
    normed = (values - centre) * lax.rsqrt(spread + 1e-06)
    modded = (normed * (1.0 + scale_row) + shift_row).astype(jnp.bfloat16)
    projected = jnp.dot(modded, head_weight, preferred_element_type=jnp.float32) + head_bias
    repeats = head_weight.shape[1] // latent_std.shape[0]
    return (projected * jnp.tile(latent_std, repeats) + jnp.tile(latent_mean, repeats)).astype(
        jnp.bfloat16
    )


def unpatch(flattened, frame_count, row_count, col_count, channels):
    blocks = flattened.reshape(frame_count, row_count, col_count, 2, 2, channels)
    blocks = jnp.transpose(blocks, (0, 1, 3, 2, 4, 5))
    return blocks.reshape(frame_count, row_count * 2, col_count * 2, channels)


def conv_input(region, weight, bias):
    frame_count = region.shape[0] - 2
    row_count = region.shape[1] - 2
    col_count = region.shape[2] - 2
    windows = []
    for time_off in range(3):
        for row_off in range(3):
            for col_off in range(3):
                windows.append(
                    region[
                        time_off : time_off + frame_count,
                        row_off : row_off + row_count,
                        col_off : col_off + col_count,
                    ]
                )
    stacked = jnp.concatenate(windows, axis=-1).reshape(frame_count * row_count * col_count, -1)
    result = jnp.dot(stacked, weight, preferred_element_type=jnp.float32) + bias
    return result.astype(jnp.bfloat16).reshape(frame_count, row_count, col_count, -1)


def activate(block_input, norm_gain):
    values = block_input.astype(jnp.float32)
    factor = lax.rsqrt(jnp.mean(values * values, axis=-1, keepdims=True) + 1e-06)
    return jax.nn.silu(values * factor * norm_gain).astype(jnp.bfloat16)


def conv_taps(padded, weight):
    batches = padded.shape[0]
    frame_count = padded.shape[1] - 2
    row_count = padded.shape[2] - 2
    col_count = padded.shape[3] - 2
    in_width = padded.shape[4]
    running = jnp.zeros(
        (batches * frame_count * row_count * col_count, weight.shape[1]), jnp.float32
    )
    for kernel_tap in range(27):
        time_off = kernel_tap // 9
        row_off = kernel_tap // 3 % 3
        col_off = kernel_tap % 3
        window = padded[
            :,
            time_off : time_off + frame_count,
            row_off : row_off + row_count,
            col_off : col_off + col_count,
        ].reshape(-1, in_width)
        running = running + jnp.dot(
            window,
            weight[kernel_tap * in_width : (kernel_tap + 1) * in_width],
            preferred_element_type=jnp.float32,
        )
    return running.reshape(batches, frame_count, row_count, col_count, weight.shape[1])


def shards(
    tokens,
    timestep,
    time_table,
    modulation,
    head_weight,
    head_bias,
    latent_std,
    latent_mean,
    conv_in_weight,
    conv_in_bias,
    norm_gain,
    conv_weight,
    conv_bias,
):
    height_devices = lax.axis_size("ha")
    width_devices = lax.axis_size("wa")
    tile_rows = PATCH * PR
    tile_cols = PATCH * PW
    channels = latent_std.shape[0]
    latent_rows = head_latent(
        tokens, timestep, time_table, modulation, head_weight, head_bias, latent_std, latent_mean
    )
    gathered = lax.all_gather(latent_rows, ("ha", "wa"), axis=0, tiled=True)
    latent_image = unpatch(gathered, F, PR * height_devices, PW * width_devices, channels)
    row_start = lax.axis_index("ha") * tile_rows
    col_start = lax.axis_index("wa") * tile_cols
    padded = jnp.pad(latent_image, ((2, 0), (1, 1), (1, 1), (0, 0)))
    region = lax.dynamic_slice(
        padded,
        (jnp.int32(0), row_start, col_start, jnp.int32(0)),
        (F + 2, tile_rows + 2, tile_cols + 2, channels),
    )
    block_input = conv_input(region, conv_in_weight, conv_in_bias)
    activated = activate(block_input, norm_gain)
    act_padded = with_halo(activated, (("ha", 1), ("wa", 2)), 1)
    act_padded = jnp.pad(act_padded, ((2, 0), (0, 0), (0, 0), (0, 0)))
    conv_sum = conv_taps(act_padded[None], lax.all_gather(conv_weight, "wa", axis=1, tiled=True))[0]
    block_mid = (conv_sum + conv_bias).astype(jnp.bfloat16)
    return (block_input, block_mid)


def solution(mesh):
    in_specs = (
        P(("clips", "ha", "wa"), None),
        P("clips"),
        P(),
        P(),
        P(),
        P(),
        P(),
        P(),
        P(),
        P(),
        P(),
        P(None, "wa"),
        P(),
    )
    out_specs = (P("clips", "ha", "wa", None), P("clips", "ha", "wa", None))
    return jax.shard_map(shards, mesh=mesh, in_specs=in_specs, out_specs=out_specs, check_vma=False)
```

profile of v0, /device:TPU:0, one launch (start us, length us, event | category | flops | bytes accessed | tf_op | source)
XLA Modules:
  0.0 113.3 jit_solution(4027090692438491039)
XLA Ops:
  7.2 0.0 copy-start
  7.2 0.0 all-gather.3.cloned.1.call-start
  7.3 0.7 all-gather.3.cloned.1.call-update
  8.9 0.7 tile.4
  9.5 0.1 mul.63
  9.6 0.7 tile.5
  10.3 0.1 add.185
  10.4 0.2 select_reduce_fusion
  10.6 0.3 convert_reduce_fusion
  10.9 0.6 fusion.2
  11.6 0.9 fusion.56
  12.5 24.6 %all-gather = bf16[16,160,64]{1,2,0:T(8,128)(2,1)S(1)} all-gather(bf16[1,160,64]{1,2,0:T(8,128)(2,1)S(1)} %fusion.56), channel_id=1, replica_groups=mesh['clips'=2,'ha'=8,'wa'=2] {'ha','wa'}, dimensions={0}, use_global_device_ids=true | all-gather | bytes 348160 | tf_op jit(solution)/shard_map/all_gather | solution.py:126
  37.0 0.3 copy.17
  37.3 0.3 reshape.140
  37.6 1.8 %copy.18 = bf16[4,8,2,80,2,16]{5,4,3,2,1,0:T(2,128)(2,1)S(1)} copy(bf16[4,8,2,80,2,16]{3,1,0,5,4,2:T(8,128)(2,1)S(1)} %bitcast.77) | data formatting | bytes 655360 | tf_op jit(solution)/shard_map/transpose | solution.py:46
  39.5 0.6 pad_dynamic-slice_fusion.3
  40.1 1.9 %pad_dynamic-slice_fusion = (bf16[4,2,80,16]{3,2,1,0:T(8,128)(2,1)}, bf16[4,2,80,16]{3,2,1,0:T(8,128)(2,1)}, bf16[4,2,80,16]{3,2,1,0:T(8,128)(2,1)}, bf16[4,2,80...) fusion(s32[]{:T(128)S(6)} %add.256, ...), kind=kLoop, calls=%fused_computation | loop fusion | bytes 552992 | tf_op jit(solution)/shard_map/slice | solution.py:59
  41.9 1.9 %pad_dynamic-slice_fusion.26 = (bf16[4,2,80,16]{3,2,1,0:T(8,128)(2,1)}, bf16[4,2,80,16]{3,2,1,0:T(8,128)(2,1)}, bf16[4,2,80,16]{3,2,1,0:T(8,128)(2,1)}, bf16[4,2...) fusion(s32[]{:T(128)S(6)} %add.256, ...), kind=kLoop, calls=%fused_computation.26 | loop fusion | bytes 552992 | tf_op jit(solution)/shard_map/slice | solution.py:59
  43.8 4.2 %concatenate.9 = bf16[4,2,80,432]{3,2,1,0:T(8,128)(2,1)S(1)} concatenate(bf16[4,2,80,16]{3,2,1,0:T(8,128)(2,1)} %get-tuple-element.3, bf16[4,2,80,16]{3,2,1,0:T(8,128)(2,1)} %get-tuple-element.4, bf16[4,2,80,16]{3,2,1,0:T(8,128)(2,1)} %get-tuple-element.14, bf16[4,2,80,16]{3,2,1,0:T(8,128)(2,1)} %get-tuple-element.5, bf16[4,2,80,16]{3,2,1,0:T(8,128)(2,1)} %get-tuple-element.6, ...), dimensions={3} | concatenate | bytes 1105920 | tf_op jit(solution)/shard_map/concatenate | solution.py:65
  48.1 0.6 multiply_reduce_fusion
  48.6 0.0 copy-start.20
  48.7 0.1 rsqrt.21
  48.8 0.4 multiply_convert_fusion
  49.1 0.1 fusion.114
  49.2 1.3 %collective-permute-start = (bf16[4,1,80,384]{3,2,1,0:T(8,128)(2,1)S(1)}, bf16[4,1,80,384]{3,2,1,0:T(8,128)(2,1)S(1)}, u32[]{:S(2)}, u32[]{:S(2)}) collective-permute-start(bf16[4,1,80,384]{3,2,1,0:T(8,128)(2,1)S(1)} %get-tuple-element.58), channel_id=1, source_target_pairs={{0,2},{2,4},{4,6},{6,8},{8,10},{10,12},{12,14},{1,3},{3,5},{5,7},{... | collective-permute-start | bytes 737288 | tf_op jit(solution)/shard_map/ppermute | solution.py:19
  50.5 1.3 %collective-permute-start.1 = (bf16[4,1,80,384]{3,2,1,0:T(8,128)(2,1)S(1)}, bf16[4,1,80,384]{3,2,1,0:T(8,128)(2,1)S(1)}, u32[]{:S(2)}, u32[]{:S(2)}) collective-permute-start(bf16[4,1,80,384]{3,2,1,0:T(8,128)(2,1)S(1)} %get-tuple-element.59), channel_id=1, source_target_pairs={{2,0},{4,2},{6,4},{8,6},{10,8},{12,10},{14,12},{3,1},{5,3},{7,5},{... | collective-permute-start | bytes 737288 | tf_op jit(solution)/shard_map/ppermute | solution.py:20
  51.8 9.9 %collective-permute-done = bf16[4,1,80,384]{3,2,1,0:T(8,128)(2,1)S(1)} collective-permute-done((bf16[4,1,80,384]{3,2,1,0:T(8,128)(2,1)S(1)}, bf16[4,1,80,384]{3,2,1,0:T(8,128)(2,1)S(1)}, u32[]{:S(2)}, u32[]{:S(2)}) %collective-permute-start) | collective-permute-done | bytes 245792 | tf_op jit(solution)/shard_map/ppermute | solution.py:19
  61.7 0.0 collective-permute-done.1
  61.8 1.7 %collective-permute-start.2 = (bf16[4,4,1,384]{3,2,1,0:T(2,128)(2,1)S(1)}, bf16[4,4,1,384]{3,2,1,0:T(2,128)(2,1)S(1)}, u32[]{:S(2)}, u32[]{:S(2)}) collective-permute-start(bf16[4,4,1,384]{3,2,1,0:T(2,128)(2,1)S(1)} %get-tuple-element.56), channel_id=1, source_target_pairs={{0,1},{2,3},{4,5},{6,7},{8,9},{10,11},{12,13},{14,15},{16,17},{18,... | collective-permute-start | bytes 36872 | tf_op jit(solution)/shard_map/ppermute | solution.py:19
  63.5 1.3 %collective-permute-start.3 = (bf16[4,4,1,384]{3,2,1,0:T(2,128)(2,1)S(1)}, bf16[4,4,1,384]{3,2,1,0:T(2,128)(2,1)S(1)}, u32[]{:S(2)}, u32[]{:S(2)}) collective-permute-start(bf16[4,4,1,384]{3,2,1,0:T(2,128)(2,1)S(1)} %get-tuple-element.57), channel_id=1, source_target_pairs={{1,0},{3,2},{5,4},{7,6},{9,8},{11,10},{13,12},{15,14},{17,16},{19,... | collective-permute-start | bytes 36872 | tf_op jit(solution)/shard_map/ppermute | solution.py:20
  64.8 0.0 collective-permute-done.2
  64.8 1.8 %collective-permute-done.3 = bf16[4,4,1,384]{3,2,1,0:T(2,128)(2,1)S(1)} collective-permute-done((bf16[4,4,1,384]{3,2,1,0:T(2,128)(2,1)S(1)}, bf16[4,4,1,384]{3,2,1,0:T(2,128)(2,1)S(1)}, u32[]{:S(2)}, u32[]{:S(2)}) %collective-permute-start.3) | collective-permute-done | bytes 12320 | tf_op jit(solution)/shard_map/ppermute | solution.py:20
  66.6 1.7 %fusion.15 = bf16[1,6,4,82,384]{4,3,2,1,0:T(8,128)(2,1)S(1)} fusion(bf16[4,4,1,384]{3,2,1,0:T(2,128)(2,1)S(1)} %collective-permute-done.3, bf16[4,4,1,384]{3,2,1,0:T(2,128)(2,1)S(1)} %collective-permute-done.2, bf16[4,1,80,384]{3,2,1,0:T(8,128)(2,1)S(1)} %collective-permute-done.1, bf16[4,2,80,384]{3,2,1,0:T(8,128)(2,1)S(1)} %multiply_convert_fusion, ...), kind=kLoop, calls=%fused_computation.44 | loop fusion | flops 12091392 | bytes 2519040 | tf_op jit(solution)/shard_map/broadcast_in_dim | solution.py:140
  68.3 2.1 %fusion.113 = (bf16[1,4,2,80,384]{4,3,2,1,0:T(8,128)(2,1)}, bf16[1,4,2,80,384]{4,3,2,1,0:T(8,128)(2,1)}, bf16[1,4,2,80,384]{4,3,2,1,0:T(8,128)(2,1)}, bf16[1,4,2...) fusion(bf16[1,6,4,82,384]{4,3,2,1,0:T(8,128)(2,1)S(1)} %fusion.15), kind=kLoop, calls=%fused_computation.147 | loop fusion | bytes 7864320 | tf_op jit(solution)/shard_map/slice | solution.py:89
  70.4 3.3 %fusion.112 = (bf16[1,4,2,80,384]{4,3,2,1,0:T(8,128)(2,1)}, bf16[1,4,2,80,384]{4,3,2,1,0:T(8,128)(2,1)}, bf16[1,4,2,80,384]{4,3,2,1,0:T(8,128)(2,1)}, bf16[1,4,2...) fusion(bf16[1,6,4,82,384]{4,3,2,1,0:T(8,128)(2,1)S(1)} %fusion.15), kind=kLoop, calls=%fused_computation.146 | loop fusion | bytes 18677760 | tf_op jit(solution)/shard_map/slice | solution.py:89
  73.7 0.0 all-gather.3.cloned.1.call-done
  73.7 1.7 %fusion.95 = f32[640,384]{1,0:T(8,128)S(1)} fusion(bf16[640,384]{1,0:T(8,128)(2,1)} %bitcast.103, bf16[10368,384]{0,1:T(8,128)(2,1)} %all-gather.3.cloned.1.call-done), kind=kOutput, calls=%fused_computation.120 | convolution fusion | flops 188743680 | bytes 1769472 | tf_op jit(solution)/shard_map/dot_general | solution.py:95
  75.5 2.3 %fusion.109 = f32[640,384]{1,0:T(8,128)S(1)} fusion(bf16[640,384]{1,0:T(8,128)(2,1)} %bitcast.102, bf16[10368,384]{0,1:T(8,128)(2,1)} %all-gather.3.cloned.1.call-done), kind=kOutput, calls=%fused_computation.134 | convolution fusion | flops 188743680 | bytes 1769472 | tf_op jit(solution)/shard_map/dot_general | solution.py:95
  77.8 1.6 %fusion.97 = f32[640,384]{1,0:T(8,128)S(1)} fusion(bf16[640,384]{1,0:T(8,128)(2,1)} %bitcast.101, bf16[10368,384]{0,1:T(8,128)(2,1)} %all-gather.3.cloned.1.call-done), kind=kOutput, calls=%fused_computation.122 | convolution fusion | flops 188743680 | bytes 1769472 | tf_op jit(solution)/shard_map/dot_general | solution.py:95
  79.4 1.6 %fusion.99 = f32[640,384]{1,0:T(8,128)S(1)} fusion(bf16[640,384]{1,0:T(8,128)(2,1)} %bitcast.100, bf16[10368,384]{0,1:T(8,128)(2,1)} %all-gather.3.cloned.1.call-done), kind=kOutput, calls=%fused_computation.124 | convolution fusion | flops 188743680 | bytes 1769472 | tf_op jit(solution)/shard_map/dot_general | solution.py:95
  81.1 1.6 %fusion.101 = f32[640,384]{1,0:T(8,128)S(1)} fusion(bf16[640,384]{1,0:T(8,128)(2,1)} %bitcast.99, bf16[10368,384]{0,1:T(8,128)(2,1)} %all-gather.3.cloned.1.call-done), kind=kOutput, calls=%fused_computation.126 | convolution fusion | flops 188743680 | bytes 1769472 | tf_op jit(solution)/shard_map/dot_general | solution.py:95
  82.8 0.5 fusion.103
  83.3 0.5 fusion.105
  83.8 0.5 fusion.107
  84.3 0.5 fusion.59
  84.8 0.5 fusion.61
  85.2 0.5 fusion.63
  85.7 0.5 fusion.65
  86.2 0.5 fusion.67
  86.7 0.5 fusion.69
  87.2 0.5 fusion.71
  87.7 0.5 fusion.73
  88.2 0.5 fusion.75
  88.7 0.5 fusion.77
  89.1 0.5 fusion.79
  89.6 0.5 fusion.81
  90.1 1.4 %fusion.83 = f32[640,384]{1,0:T(8,128)} fusion(bf16[640,384]{1,0:T(8,128)(2,1)S(1)} %bitcast.83, bf16[10368,384]{0,1:T(8,128)(2,1)S(1)} %copy-done.2), kind=kOutput, calls=%fused_computation.108 | convolution fusion | flops 188743680 | bytes 1769472 | tf_op jit(solution)/shard_map/dot_general | solution.py:95
  91.6 1.4 %fusion.85 = f32[640,384]{1,0:T(8,128)} fusion(bf16[640,384]{1,0:T(8,128)(2,1)S(1)} %bitcast.82, bf16[10368,384]{0,1:T(8,128)(2,1)S(1)} %copy-done.2), kind=kOutput, calls=%fused_computation.110 | convolution fusion | flops 188743680 | bytes 1769472 | tf_op jit(solution)/shard_map/dot_general | solution.py:95
  93.0 1.4 %fusion.87 = f32[640,384]{1,0:T(8,128)} fusion(bf16[640,384]{1,0:T(8,128)(2,1)S(1)} %bitcast.81, bf16[10368,384]{0,1:T(8,128)(2,1)S(1)} %copy-done.2), kind=kOutput, calls=%fused_computation.112 | convolution fusion | flops 188743680 | bytes 1769472 | tf_op jit(solution)/shard_map/dot_general | solution.py:95
  94.4 1.4 %fusion.89 = f32[640,384]{1,0:T(8,128)} fusion(bf16[640,384]{1,0:T(8,128)(2,1)S(1)} %bitcast.80, bf16[10368,384]{0,1:T(8,128)(2,1)S(1)} %copy-done.2), kind=kOutput, calls=%fused_computation.114 | convolution fusion | flops 188743680 | bytes 1769472 | tf_op jit(solution)/shard_map/dot_general | solution.py:95
  95.8 1.4 %fusion.91 = f32[640,384]{1,0:T(8,128)} fusion(bf16[640,384]{1,0:T(8,128)(2,1)S(1)} %bitcast.79, bf16[10368,384]{0,1:T(8,128)(2,1)S(1)} %copy-done.2), kind=kOutput, calls=%fused_computation.116 | convolution fusion | flops 188743680 | bytes 1769472 | tf_op jit(solution)/shard_map/dot_general | solution.py:95
  97.3 1.5 %fusion.93 = f32[640,384]{1,0:T(8,128)} fusion(bf16[640,384]{1,0:T(8,128)(2,1)S(1)} %bitcast.78, bf16[10368,384]{0,1:T(8,128)(2,1)S(1)} %copy-done.2), kind=kOutput, calls=%fused_computation.118 | convolution fusion | flops 188743680 | bytes 1769472 | tf_op jit(solution)/shard_map/dot_general | solution.py:95
  98.7 5.7 %fusion.42 = f32[640,384]{1,0:T(8,128)} fusion(f32[640,384]{1,0:T(8,128)S(1)} %fusion.59, f32[640,384]{1,0:T(8,128)S(1)} %fusion.61, f32[640,384]{1,0:T(8,128)S(1)} %fusion.63, f32[640,384]{1,0:T(8,128)S(1)} %fusion.65, f32[640,384]{1,0:T(8,128)S(1)} %fusion.67, f32[640,384]{1,0:T(8,128)S(1)} %fusion.69, f32[640,384]{1,0:T(8,128)S(1)} %fusion.71, ...), kind=kOutput, calls=%fused_computation.73 | convolution fusion | flops 195133440 | bytes 27328512 | tf_op jit(solution)/shard_map/dot_general | solution.py:95
  104.4 2.0 %add_convert_fusion = bf16[4,2,80,384]{3,2,1,0:T(8,128)(2,1)} fusion(f32[4,2,80,384]{3,2,1,0:T(8,128)} %bitcast.76, f32[384]{0:T(512)S(1)} %copy-done.23), kind=kLoop, calls=%fused_computation.81 | loop fusion | flops 491520 | bytes 1476096 | tf_op jit(solution)/shard_map/convert_element_type | solution.py:141
  (58 shorter events, 0.2 us)
Async XLA Ops:
  7.2 4.4 %copy-start = (bf16[5120,64]{0,1:T(8,128)(2,1)S(1)}, bf16[5120,64]{0,1:T(8,128)(2,1)}, u32[]{:S(2)}) copy-start(bf16[5120,64]{0,1:T(8,128)(2,1)} %param.17) | copy-start | bytes 1966084
  7.2 3.2 %copy-start.19 = (f32[50,5120]{1,0:T(8,128)S(1)}, f32[50,5120]{1,0:T(8,128)}, u32[]{:S(2)}) copy-start(f32[50,5120]{1,0:T(8,128)} %param.15) | copy-start | bytes 3072004
  7.2 3.4 %copy-start.3 = (bf16[160,5120]{1,0:T(8,128)(2,1)S(1)}, bf16[160,5120]{1,0:T(8,128)(2,1)}, u32[]{:S(2)}) copy-start(bf16[160,5120]{1,0:T(8,128)(2,1)} %param.13) | copy-start | bytes 4915204
  7.2 4.3 %copy-start.21 = (f32[2,5120]{1,0:T(2,128)S(1)}, f32[2,5120]{1,0:T(2,128)}, u32[]{:S(2)}) copy-start(f32[2,5120]{1,0:T(2,128)} %param.16) | copy-start | bytes 122884
  7.2 4.3 %copy-start.26 = (f32[64]{0:T(128)S(1)}, f32[64]{0:T(128)}, u32[]{:S(2)}) copy-start(f32[64]{0:T(128)} %param.18) | copy-start | bytes 772
  7.2 66.5 %all-gather.3.cloned.1.call-start = ((), (), s32[]{:S(2)}) async-start(), calls=%async_computation | async-start | bytes 11943936 | tf_op jit(solution)/shard_map/all_gather | solution.py:140
  41.9 6.1 %copy-start.25 = (f32[384]{0:T(512)S(1)}, f32[384]{0:T(512)}, u32[]{:S(2)}) copy-start(f32[384]{0:T(512)} %param.22) | copy-start | bytes 4612
  43.8 4.2 %copy-start.24 = (bf16[432,384]{1,0:T(8,128)(2,1)S(1)}, bf16[432,384]{1,0:T(8,128)(2,1)}, u32[]{:S(2)}) copy-start(bf16[432,384]{1,0:T(8,128)(2,1)} %param.21) | copy-start | bytes 995332
  43.8 4.9 %copy-start.22 = (f32[384]{0:T(512)S(1)}, f32[384]{0:T(512)}, u32[]{:S(2)}) copy-start(f32[384]{0:T(512)} %param.23) | copy-start | bytes 4612
  48.6 19.7 %copy-start.20 = (bf16[640,384]{1,0:T(8,128)(2,1)}, bf16[640,384]{1,0:T(8,128)(2,1)S(1)}, u32[]{:S(2)}) copy-start(bf16[640,384]{1,0:T(8,128)(2,1)S(1)} %get-tuple-element.63) | copy-start | bytes 1474564
  49.2 12.6 %collective-permute-start = (bf16[4,1,80,384]{3,2,1,0:T(8,128)(2,1)S(1)}, bf16[4,1,80,384]{3,2,1,0:T(8,128)(2,1)S(1)}, u32[]{:S(2)}, u32[]{:S(2)}) collective-permute-start(bf16[4,1,80,384]{3,2,1,0:T(8,128)(2,1)S(1)} %get-tuple-element.58), channel_id=1, source_target_pairs={{0,2},{2,4},{4,6},{6,8},{8,10},{10,12},{12,14},{1,3},{3,5},{5,7},{... | collective-permute-start | bytes 737288 | tf_op jit(solution)/shard_map/ppermute | solution.py:19
  50.5 11.2 %collective-permute-start.1 = (bf16[4,1,80,384]{3,2,1,0:T(8,128)(2,1)S(1)}, bf16[4,1,80,384]{3,2,1,0:T(8,128)(2,1)S(1)}, u32[]{:S(2)}, u32[]{:S(2)}) collective-permute-start(bf16[4,1,80,384]{3,2,1,0:T(8,128)(2,1)S(1)} %get-tuple-element.59), channel_id=1, source_target_pairs={{2,0},{4,2},{6,4},{8,6},{10,8},{12,10},{14,12},{3,1},{5,3},{7,5},{... | collective-permute-start | bytes 737288 | tf_op jit(solution)/shard_map/ppermute | solution.py:20
  61.8 3.0 %collective-permute-start.2 = (bf16[4,4,1,384]{3,2,1,0:T(2,128)(2,1)S(1)}, bf16[4,4,1,384]{3,2,1,0:T(2,128)(2,1)S(1)}, u32[]{:S(2)}, u32[]{:S(2)}) collective-permute-start(bf16[4,4,1,384]{3,2,1,0:T(2,128)(2,1)S(1)} %get-tuple-element.56), channel_id=1, source_target_pairs={{0,1},{2,3},{4,5},{6,7},{8,9},{10,11},{12,13},{14,15},{16,17},{18,... | collective-permute-start | bytes 36872 | tf_op jit(solution)/shard_map/ppermute | solution.py:19
  63.5 3.1 %collective-permute-start.3 = (bf16[4,4,1,384]{3,2,1,0:T(2,128)(2,1)S(1)}, bf16[4,4,1,384]{3,2,1,0:T(2,128)(2,1)S(1)}, u32[]{:S(2)}, u32[]{:S(2)}) collective-permute-start(bf16[4,4,1,384]{3,2,1,0:T(2,128)(2,1)S(1)} %get-tuple-element.57), channel_id=1, source_target_pairs={{1,0},{3,2},{5,4},{7,6},{9,8},{11,10},{13,12},{15,14},{17,16},{19,... | collective-permute-start | bytes 36872 | tf_op jit(solution)/shard_map/ppermute | solution.py:20
  73.7 9.0 %copy-start.2 = (bf16[10368,384]{0,1:T(8,128)(2,1)S(1)}, bf16[10368,384]{0,1:T(8,128)(2,1)}, u32[]{:S(2)}) copy-start(bf16[10368,384]{0,1:T(8,128)(2,1)} %all-gather.3.cloned.1.call-done) | copy-start | bytes 23887876
  73.7 9.0 %copy-start.18 = (bf16[1,4,2,80,384]{4,3,2,1,0:T(8,128)(2,1)S(1)}, bf16[1,4,2,80,384]{4,3,2,1,0:T(8,128)(2,1)}, u32[]{:S(2)}) copy-start(bf16[1,4,2,80,384]{4,3,2,1,0:T(8,128)(2,1)} %get-tuple-element.53) | copy-start | bytes 1474564
  75.5 7.8 %copy-start.17 = (bf16[1,4,2,80,384]{4,3,2,1,0:T(8,128)(2,1)S(1)}, bf16[1,4,2,80,384]{4,3,2,1,0:T(8,128)(2,1)}, u32[]{:S(2)}) copy-start(bf16[1,4,2,80,384]{4,3,2,1,0:T(8,128)(2,1)} %get-tuple-element.54) | copy-start | bytes 1474564
  77.8 6.0 %copy-start.16 = (bf16[1,4,2,80,384]{4,3,2,1,0:T(8,128)(2,1)S(1)}, bf16[1,4,2,80,384]{4,3,2,1,0:T(8,128)(2,1)}, u32[]{:S(2)}) copy-start(bf16[1,4,2,80,384]{4,3,2,1,0:T(8,128)(2,1)} %get-tuple-element.55) | copy-start | bytes 1474564
  79.4 4.8 %copy-start.15 = (bf16[1,4,2,80,384]{4,3,2,1,0:T(8,128)(2,1)S(1)}, bf16[1,4,2,80,384]{4,3,2,1,0:T(8,128)(2,1)}, u32[]{:S(2)}) copy-start(bf16[1,4,2,80,384]{4,3,2,1,0:T(8,128)(2,1)} %get-tuple-element.30) | copy-start | bytes 1474564
  81.1 3.7 %copy-start.14 = (bf16[1,4,2,80,384]{4,3,2,1,0:T(8,128)(2,1)S(1)}, bf16[1,4,2,80,384]{4,3,2,1,0:T(8,128)(2,1)}, u32[]{:S(2)}) copy-start(bf16[1,4,2,80,384]{4,3,2,1,0:T(8,128)(2,1)} %get-tuple-element.31) | copy-start | bytes 1474564
  82.7 2.5 %copy-start.13 = (bf16[1,4,2,80,384]{4,3,2,1,0:T(8,128)(2,1)S(1)}, bf16[1,4,2,80,384]{4,3,2,1,0:T(8,128)(2,1)}, u32[]{:S(2)}) copy-start(bf16[1,4,2,80,384]{4,3,2,1,0:T(8,128)(2,1)} %get-tuple-element.32) | copy-start | bytes 1474564
  83.2 2.5 %copy-start.12 = (bf16[1,4,2,80,384]{4,3,2,1,0:T(8,128)(2,1)S(1)}, bf16[1,4,2,80,384]{4,3,2,1,0:T(8,128)(2,1)}, u32[]{:S(2)}) copy-start(bf16[1,4,2,80,384]{4,3,2,1,0:T(8,128)(2,1)} %get-tuple-element.33) | copy-start | bytes 1474564
  83.7 2.5 %copy-start.11 = (bf16[1,4,2,80,384]{4,3,2,1,0:T(8,128)(2,1)S(1)}, bf16[1,4,2,80,384]{4,3,2,1,0:T(8,128)(2,1)}, u32[]{:S(2)}) copy-start(bf16[1,4,2,80,384]{4,3,2,1,0:T(8,128)(2,1)} %get-tuple-element.34) | copy-start | bytes 1474564
  84.2 2.5 %copy-start.10 = (bf16[1,4,2,80,384]{4,3,2,1,0:T(8,128)(2,1)S(1)}, bf16[1,4,2,80,384]{4,3,2,1,0:T(8,128)(2,1)}, u32[]{:S(2)}) copy-start(bf16[1,4,2,80,384]{4,3,2,1,0:T(8,128)(2,1)} %get-tuple-element.35) | copy-start | bytes 1474564
  84.7 2.5 %copy-start.9 = (bf16[1,4,2,80,384]{4,3,2,1,0:T(8,128)(2,1)S(1)}, bf16[1,4,2,80,384]{4,3,2,1,0:T(8,128)(2,1)}, u32[]{:S(2)}) copy-start(bf16[1,4,2,80,384]{4,3,2,1,0:T(8,128)(2,1)} %get-tuple-element.36) | copy-start | bytes 1474564
  87.2 2.4 %copy-start.8 = (bf16[1,4,2,80,384]{4,3,2,1,0:T(8,128)(2,1)S(1)}, bf16[1,4,2,80,384]{4,3,2,1,0:T(8,128)(2,1)}, u32[]{:S(2)}) copy-start(bf16[1,4,2,80,384]{4,3,2,1,0:T(8,128)(2,1)} %get-tuple-element.41) | copy-start | bytes 1474564
  87.7 2.4 %copy-start.7 = (bf16[1,4,2,80,384]{4,3,2,1,0:T(8,128)(2,1)S(1)}, bf16[1,4,2,80,384]{4,3,2,1,0:T(8,128)(2,1)}, u32[]{:S(2)}) copy-start(bf16[1,4,2,80,384]{4,3,2,1,0:T(8,128)(2,1)} %get-tuple-element.42) | copy-start | bytes 1474564
  88.2 3.4 %copy-start.6 = (bf16[1,4,2,80,384]{4,3,2,1,0:T(8,128)(2,1)S(1)}, bf16[1,4,2,80,384]{4,3,2,1,0:T(8,128)(2,1)}, u32[]{:S(2)}) copy-start(bf16[1,4,2,80,384]{4,3,2,1,0:T(8,128)(2,1)} %get-tuple-element.43) | copy-start | bytes 1474564
  88.6 4.3 %copy-start.5 = (bf16[1,4,2,80,384]{4,3,2,1,0:T(8,128)(2,1)S(1)}, bf16[1,4,2,80,384]{4,3,2,1,0:T(8,128)(2,1)}, u32[]{:S(2)}) copy-start(bf16[1,4,2,80,384]{4,3,2,1,0:T(8,128)(2,1)} %get-tuple-element.44) | copy-start | bytes 1474564
  89.1 5.3 %copy-start.4 = (bf16[1,4,2,80,384]{4,3,2,1,0:T(8,128)(2,1)S(1)}, bf16[1,4,2,80,384]{4,3,2,1,0:T(8,128)(2,1)}, u32[]{:S(2)}) copy-start(bf16[1,4,2,80,384]{4,3,2,1,0:T(8,128)(2,1)} %get-tuple-element.45) | copy-start | bytes 1474564
  98.7 5.7 %copy-start.23 = (f32[384]{0:T(512)S(1)}, f32[384]{0:T(512)}, u32[]{:S(2)}) copy-start(f32[384]{0:T(512)} %param.25) | copy-start | bytes 4612
  98.7 7.8 %copy-start.1 = (bf16[5120,64]{0,1:T(8,128)(2,1)S(1)}, bf16[5120,64]{0,1:T(8,128)(2,1)}, u32[]{:S(2)}) copy-start(bf16[5120,64]{0,1:T(8,128)(2,1)} %param.17) | copy-start | bytes 1966084
Sparse Core Ops, SparseCore 0:
  9.6 22.0 all-gather.2
where the time goes:
time: 114 us; the launch traced here: 113 us
  matrix products  31.7 us (28%)
  blocking collectives  24.6 us (22%)
  local copies, waits for them, and re-layouts  18.1 us (16%)
  between operations  15.6 us (14%)
  waiting for transfers between devices  12.4 us (11%)
  starting transfers between devices  5.61 us (5%)
  other arithmetic  5.35 us (5%)
    dot_general x27, matrix products, conv_taps(): jnp.dot(window, weight[kernel_tap * in_width:(kernel_tap + 1) * in_width]...  30.3 us
    all_gather x1, blocking collectives, shards(): gathered = lax.all_gather(latent_rows, ('ha', 'wa'), axis=0, tiled=True)  24.6 us
    ppermute x2, waiting for transfers between devices, with_halo(): before = lax.ppermute(last, axis, up)  9.95 us
    slice x2, local copies, waits for them, and re-layouts, conv_taps(): padded[:, time_off:time_off + frame_count, row_off:row_off + row_count, c...  5.36 us
    slice x3, local copies, waits for them, and re-layouts, conv_input(): region[time_off:time_off + frame_count, row_off:row_off + row_count, col_...  4.34 us
    concatenate x1, local copies, waits for them, and re-layouts, conv_input(): jnp.concatenate(windows, axis=-1)  4.2 us
    ppermute x2, starting transfers between devices, with_halo(): before = lax.ppermute(last, axis, up)  2.99 us
    ppermute x2, starting transfers between devices, with_halo(): after = lax.ppermute(first, axis, down)  2.58 us
  transfers between devices with their start and end apart: 5, of which 2 were waited for; matrix products, arithmetic and copies ran while one was open for 20% of the time, Pallas kernels for 0%

commit v1 on v0

v1 whole, which is shorter than its diff:
```python
import functools

import jax
import jax.numpy as jnp
from jax import lax
from jax.experimental import pallas as pl
from jax.experimental.pallas import tpu as pltpu
from jax.sharding import PartitionSpec as P

F = 4
PW = 40
MESH = pl.DeviceIdType.MESH
CP = 96
F32 = jnp.float32
BF16 = jnp.bfloat16
CHUNK = 32


def dot_t(lhs, rhs):
    return lax.dot_general(lhs, rhs, (((1,), (1,)), ((), ())), preferred_element_type=F32)


def kernel(
    heights,
    widths,
    tok_hbm,
    ts_ref,
    table_hbm,
    mod_ref,
    hw_hbm,
    hb_ref,
    std_ref,
    mean_ref,
    ciw_ref,
    cib_ref,
    gain_ref,
    w_hbm,
    cb_ref,
    out1,
    out2,
    tok,
    table,
    hw,
    w,
    modded,
    lat,
    recv,
    zbuf,
    pair,
    wc,
    ybuf,
    xbuf,
    act,
    acc,
    res,
    peer_res,
    stage,
    tok_sem,
    in_sem,
    send_sem,
    recv_sem,
    peer_sem,
):
    ha = lax.axis_index("ha")
    wa = lax.axis_index("wa")
    me = ha * widths + wa
    quarter = heights * widths // F
    frame = me // quarter
    pp = me % quarter
    rows = tok.shape[0]
    cols = rows // 2
    chan = gain_ref.shape[1]
    half_chan = w.shape[0]
    zch = std_ref.shape[1]
    odd = ha % 2

    table_copy = pltpu.make_async_copy(table_hbm, table, in_sem.at[0])
    table_copy.start()

    def tok_copy(i):
        part = pl.ds(pl.multiple_of(i * CHUNK, CHUNK), CHUNK)
        return pltpu.make_async_copy(tok_hbm.at[part], tok.at[part], tok_sem.at[i])

    for i in range(rows // CHUNK):
        tok_copy(i).start()
    hw_copy = pltpu.make_async_copy(hw_hbm, hw, in_sem.at[1])
    hw_copy.start()
    w_copy = pltpu.make_async_copy(w_hbm, w, in_sem.at[2])
    w_copy.start()

    base = ha // 2

    def source(ff, kind):
        if kind == 0:
            return ff * quarter + base, ha >= 0
        return ff * quarter + base + 2 * odd - 1, (ha + 2 * odd - 1 >= 0) & (
            ha + 2 * odd - 1 < heights
        )

    barrier = pltpu.get_barrier_semaphore()
    for ff in range(F):
        for kind in range(2):
            device, exists = source(ff, kind)

            @pl.when(exists & (device != me))
            def _():
                pl.semaphore_signal(
                    barrier,
                    inc=1,
                    device_id={"ha": device // widths, "wa": device % widths},
                    device_id_type=MESH,
                )

    pl.semaphore_signal(barrier, inc=1, device_id={"wa": 1 - wa}, device_id_type=MESH)

    table_copy.wait()
    embed = table[pl.ds(ts_ref[0], 1), :]
    shift = mod_ref[0:1, :] + embed
    scale = 1.0 + (mod_ref[1:2, :] + embed)

    def head_step(i, carry):
        tok_copy(i).wait()
        for j in range(CHUNK // 16):
            part = pl.ds(pl.multiple_of(i * CHUNK + j * 16, 16), 16)
            values = tok[part, :].astype(F32)
            centre = jnp.mean(values, axis=-1, keepdims=True)
            delta = values - centre
            spread = jnp.mean(delta * delta, axis=-1, keepdims=True)
            modded[part, :] = (delta * lax.rsqrt(spread + 1e-06) * scale + shift).astype(BF16)
        return carry

    lax.fori_loop(0, rows // CHUNK, head_step, 0)
    hw_copy.wait()
    projected = dot_t(modded[...], hw[...]) + hb_ref[...]
    repeats = hw.shape[0] // zch
    projected = projected * jnp.concatenate([std_ref[...]] * repeats, axis=1) + jnp.concatenate(
        [mean_ref[...]] * repeats, axis=1
    )
    lat[...] = (
        jnp.concatenate([projected, projected], axis=1).astype(BF16).reshape(2, cols, lat.shape[2])
    )

    plan = ((0, 1, 2, 1), (0, 2, 1, 0), (0, 2, 0, 0), (1, 1, 0, 1))

    def targets():
        for k, (row, count, slot, kind) in enumerate(plan):
            to_ha = 2 * pp - 1 + k
            for to_wa in range(2):
                valid = (to_ha >= 0) & (to_ha < heights)
                mine = (to_ha == ha) & (wa == to_wa)
                copy = pltpu.make_async_remote_copy(
                    src_ref=lat.at[pl.ds(row, count)],
                    dst_ref=recv.at[frame, pl.ds(slot, count)],
                    send_sem=send_sem.at[k, to_wa],
                    recv_sem=recv_sem.at[frame, kind],
                    device_id={"ha": to_ha, "wa": to_wa},
                    device_id_type=MESH,
                )
                yield valid, mine, copy, row, count, slot

    expected = jnp.int32(1)
    for k in range(4):
        to_ha = 2 * pp - 1 + k
        valid = (to_ha >= 0) & (to_ha < heights)
        expected += jnp.where(valid, 2 - jnp.where(to_ha == ha, 1, 0), 0)
    pl.semaphore_wait(barrier, expected)
    for valid, mine, copy, row, count, slot in targets():

        @pl.when(valid & jnp.logical_not(mine))
        def _():
            copy.start()

        @pl.when(valid & mine)
        def _():
            recv[frame, slot : slot + count] = lat[row : row + count]

    wc[...] = jnp.zeros(wc.shape, BF16)
    for a in range(3):
        for win_row in range(4):
            for win_col in range(4):
                k0 = a * 256 + ((win_row // 2) * 2 + win_col // 2) * 64
                k0 += ((win_row % 2) * 2 + win_col % 2) * zch
                for o_row in range(2):
                    for o_col in range(2):
                        b, e = win_row - o_row, win_col - o_col
                        if 0 <= b < 3 and 0 <= e < 3:
                            r0 = ((3 * a + b) * 3 + e) * zch
                            c0 = (o_row * 2 + o_col) * chan
                            wc[k0 : k0 + zch, c0 : c0 + chan] = ciw_ref[r0 : r0 + zch, :]

    @pl.when(ha == 0)
    def _():
        recv[:, 0] = jnp.zeros((F,) + recv.shape[2:], BF16)

    @pl.when(ha == heights - 1)
    def _():
        recv[:, 2] = jnp.zeros((F,) + recv.shape[2:], BF16)

    zbuf[...] = jnp.zeros(zbuf.shape, F32)
    lane = lax.broadcasted_iota(jnp.int32, (CP, 128), 1)
    position = lax.broadcasted_iota(jnp.int32, (88, 1), 0)
    bias_in = jnp.concatenate([cib_ref[...]] * 4, axis=1)
    gain = gain_ref[...]
    first = wa == 0

    for ff in range(F):
        for kind in range(2):
            device, exists = source(ff, kind)
            slot = (1 - odd) if kind == 0 else 2 * odd

            @pl.when(exists & (device != me))
            def _():
                pltpu.make_async_remote_copy(
                    src_ref=lat.at[pl.ds(0, 2 - kind)],
                    dst_ref=recv.at[ff, pl.ds(slot, 2 - kind)],
                    send_sem=send_sem.at[0, 0],
                    recv_sem=recv_sem.at[ff, kind],
                    device_id={"wa": 1 - wa},
                    device_id_type=MESH,
                ).wait_recv()

        for t in range(3):
            zbuf[8 : 8 + cols, :] = recv[ff, t].astype(F32)
            left = zbuf[7 : 7 + CP, :]
            right = zbuf[8 : 8 + CP, :]
            pair[ff, t] = jnp.where(lane < 64, left, right).astype(BF16)

        pieces = []
        for a in range(max(0, 2 - ff), 3):
            for ti in range(2):
                pieces.append(pair[ff + a - 2, ti : ti + 2].reshape(2 * CP, 128))
        lhs = jnp.concatenate(pieces, axis=1)
        ybuf[...] = (
            (
                jnp.dot(lhs, wc[wc.shape[0] - lhs.shape[1] :, :], preferred_element_type=F32)
                + bias_in
            )
            .astype(BF16)
            .astype(F32)
        )
        for i in range(2):
            for o_row in range(2):
                row = 2 * i + o_row
                for o_col in range(2):
                    c0 = (o_row * 2 + o_col) * chan
                    v = ybuf[i * CP : i * CP + 88, c0 : c0 + chan]
                    factor = lax.rsqrt(jnp.mean(v * v, axis=-1, keepdims=True) + 1e-06)
                    z = v * factor * gain
                    s = z / (1.0 + jnp.exp(-z))
                    keep = (position > 0) if o_col == 0 else (position < cols)
                    if row == 0:
                        keep = keep & (ha > 0)
                    if row == 3:
                        keep = keep & (ha < heights - 1)
                    xbuf[o_col] = jnp.where(keep, s, 0.0)
                for h in range(2):
                    lo = h * PW
                    x0 = xbuf[0, lo : lo + PW, :]
                    x1 = xbuf[1, lo : lo + PW, :]
                    x0s = xbuf[0, lo + 1 : lo + 1 + PW, :]
                    x1s = xbuf[1, lo + 1 : lo + 1 + PW, :]
                    act[ff, row, h, :, 0:chan] = jnp.concatenate([x0, x1], axis=0).astype(BF16)
                    act[ff, row, h, :, chan : 2 * chan] = jnp.concatenate(
                        [x1, x0s], axis=0
                    ).astype(BF16)
                    act[ff, row, h, :, 2 * chan : 3 * chan] = jnp.concatenate(
                        [x0s, x1s], axis=0
                    ).astype(BF16)
                if row in (1, 2):
                    c0 = o_row * 2 * chan
                    c1 = c0 + chan
                    r0 = i * CP
                    even = jnp.where(
                        first, ybuf[r0 : r0 + PW, c1 : c1 + chan], ybuf[r0 + PW : r0 + 2 * PW, c1 : c1 + chan]
                    )
                    after = jnp.where(
                        first,
                        ybuf[r0 + 1 : r0 + 1 + PW, c0:c1],
                        ybuf[r0 + 1 + PW : r0 + 1 + 2 * PW, c0:c1],
                    )
                    for q in range(chan // 128):
                        part = slice(q * 128, q * 128 + 128)
                        stage[q, pl.ds(0, PW, stride=2), :] = even[:, part]
                        stage[q, pl.ds(1, PW, stride=2), :] = after[:, part]
                        out1[ff, row - 1, :, part] = stage[q].astype(BF16)

    for valid, mine, copy, row, count, slot in targets():

        @pl.when(valid & jnp.logical_not(mine))
        def _():
            copy.wait_send()

    w_copy.wait()
    bias = jnp.where(first, cb_ref[:, 0:half_chan], cb_ref[:, half_chan : 2 * half_chan])
    peer_copy = pltpu.make_async_remote_copy(
        src_ref=res.at[0],
        dst_ref=peer_res,
        send_sem=peer_sem.at[0],
        recv_sem=peer_sem.at[1],
        device_id={"wa": 1 - wa},
        device_id_type=MESH,
    )

    depth = 3 * chan
    block = 2 * 2 * PW

    def half_step(step, carry):
        h = jnp.where(step == 0, 1 - wa, wa)
        for a in (2, 1, 0):
            frames = 2 + a
            for b in range(3):
                lhs = act[0:frames, b : b + 2, h].reshape(frames * block, depth)
                k0 = (3 * a + b) * depth
                term = dot_t(lhs, w[:, k0 : k0 + depth])
                if a == 2 and b == 0:
                    acc[...] = term
                else:
                    acc[(F - frames) * block :, :] += term
        res[step] = (acc[...] + bias).astype(BF16).reshape(res.shape[1:])

        @pl.when(step == 0)
        def _():
            peer_copy.start()

        return carry

    lax.fori_loop(0, 2, half_step, 0)
    peer_copy.wait()
    for ff in range(F):
        for row in range(2):
            own = res[1, ff, row].astype(F32)
            other = peer_res[ff, row].astype(F32)
            full = jnp.concatenate(
                [jnp.where(first, own, other), jnp.where(first, other, own)], axis=1
            )
            for q in range(chan // 128):
                part = slice(q * 128, q * 128 + 128)
                stage[q, pl.ds(0, PW, stride=2), :] = full[0:PW, part]
                stage[q, pl.ds(1, PW, stride=2), :] = full[PW : 2 * PW, part]
                out2[ff, row, :, part] = stage[q].astype(BF16)


def shards(
    tokens,
    timestep,
    time_table,
    modulation,
    head_weight,
    head_bias,
    latent_std,
    latent_mean,
    conv_in_weight,
    conv_in_bias,
    norm_gain,
    conv_weight,
    conv_bias,
):
    heights = lax.axis_size("ha")
    widths = lax.axis_size("wa")
    rows, width = tokens.shape
    cols = rows // 2
    chan = norm_gain.shape[0]
    half_chan = conv_weight.shape[1]
    whole = pl.BlockSpec(memory_space=pltpu.VMEM)
    far = pl.BlockSpec(memory_space=pl.ANY)
    out = jax.ShapeDtypeStruct((F, 2, 2 * PW, chan), BF16)
    return tuple(
        pl.pallas_call(
            functools.partial(kernel, heights, widths),
            out_shape=(out, out),
            in_specs=[
                far,
                pl.BlockSpec(memory_space=pltpu.SMEM),
                far,
                whole,
                far,
                whole,
                whole,
                whole,
                whole,
                whole,
                whole,
                far,
                whole,
            ],
            out_specs=(whole, whole),
            scratch_shapes=[
                pltpu.VMEM((rows, width), BF16),
                pltpu.VMEM(time_table.shape, F32),
                pltpu.VMEM(head_weight.shape[::-1], BF16),
                pltpu.VMEM(conv_weight.shape[::-1], BF16),
                pltpu.VMEM((rows, width), BF16),
                pltpu.VMEM((2, cols, 128), BF16),
                pltpu.VMEM((F, 3, cols, 128), BF16),
                pltpu.VMEM((CP + 16, 128), F32),
                pltpu.VMEM((F, 3, CP, 128), BF16),
                pltpu.VMEM((768, 4 * chan), BF16),
                pltpu.VMEM((2 * CP, 4 * chan), F32),
                pltpu.VMEM((2, 88, chan), F32),
                pltpu.VMEM((F, 4, 2, 2 * PW, 3 * chan), BF16),
                pltpu.VMEM((F * 4 * PW, half_chan), F32),
                pltpu.VMEM((2, F, 2, 2 * PW, half_chan), BF16),
                pltpu.VMEM((F, 2, 2 * PW, half_chan), BF16),
                pltpu.VMEM((chan // 128, 2 * PW, 128), F32),
                pltpu.SemaphoreType.DMA((rows // CHUNK,)),
                pltpu.SemaphoreType.DMA((3,)),
                pltpu.SemaphoreType.DMA((4, 2)),
                pltpu.SemaphoreType.DMA((F, 2)),
                pltpu.SemaphoreType.DMA((2,)),
            ],
            compiler_params=pltpu.CompilerParams(
                collective_id=0, has_side_effects=True, vmem_limit_bytes=50 << 20
            ),
        )(
            tokens,
            timestep,
            time_table,
            modulation,
            head_weight.T,
            head_bias[None],
            latent_std[None],
            latent_mean[None],
            conv_in_weight,
            conv_in_bias[None],
            norm_gain[None],
            conv_weight.T,
            conv_bias[None],
        )
    )


def solution(mesh):
    in_specs = (
        P(("clips", "ha", "wa"), None),
        P("clips"),
        P(),
        P(),
        P(),
        P(),
        P(),
        P(),
        P(),
        P(),
        P(),
        P(None, "wa"),
        P(),
    )
    out_specs = (P("clips", "ha", "wa", None), P("clips", "ha", "wa", None))
    return jax.shard_map(shards, mesh=mesh, in_specs=in_specs, out_specs=out_specs, check_vma=False)
```

time: 114 us -> 36.4 us (0.32)
  the two profiles are of different devices: /device:TPU:0 before, /device:TPU:25 now
where the time goes in v1:
time: 36.4 us; the launch traced here: 36 us
  Pallas kernels  25.1 us (69%)
  local copies, waits for them, and re-layouts  9.67 us (27%)
  between operations  1.29 us (4%)
    pallas_call x1, Pallas kernels, shards(): pl.pallas_call(functools.partial(kernel, heights, widths), out_shape=(out...  25.1 us
    unnamed x16, local copies, waits for them, and re-layouts  7.62 us

profile of v1, /device:TPU:25, one launch (start us, length us, event | category | flops | bytes accessed | tf_op | source)
XLA Modules:
  0.0 36.0 jit_solution(6085436039314679445)
XLA Ops:
  1.3 0.7 %broadcast_in_dim.21.cib_ref = f32[1,384]{1,0:T(1,128)S(1)} reshape(f32[384]{0:T(512)} %param.22) | data formatting | bytes 3072 | tf_op jit(solution)/shard_map/broadcast_in_dim | solution.py:424
  2.0 0.7 %broadcast_in_dim.22.gain_ref = f32[1,384]{1,0:T(1,128)S(1)} reshape(f32[384]{0:T(512)} %param.23) | data formatting | bytes 3072 | tf_op jit(solution)/shard_map/broadcast_in_dim | solution.py:425
  2.6 0.7 %broadcast_in_dim.23.cb_ref = f32[1,384]{1,0:T(1,128)S(1)} reshape(f32[384]{0:T(512)} %param.25) | data formatting | bytes 3072 | tf_op jit(solution)/shard_map/broadcast_in_dim | solution.py:427
  3.3 0.0 copy-start
  3.3 1.3 %copy-done = f32[50,5120]{1,0:T(8,128)S(1)} copy-done((f32[50,5120]{1,0:T(8,128)S(1)}, f32[50,5120]{1,0:T(8,128)}, u32[]{:S(2)}) %copy-start) | copy-done | bytes 1024024
  4.6 0.0 copy-start.1
  4.6 1.1 %copy-done.1 = bf16[5120,64]{0,1:T(8,128)(2,1)S(1)} copy-done((bf16[5120,64]{0,1:T(8,128)(2,1)S(1)}, bf16[5120,64]{0,1:T(8,128)(2,1)}, u32[]{:S(2)}) %copy-start.1) | copy-done | bytes 655384
  5.7 0.0 copy-start.2
  5.7 1.0 %copy-done.2 = bf16[432,384]{1,0:T(8,128)(2,1)S(1)} copy-done((bf16[432,384]{1,0:T(8,128)(2,1)S(1)}, bf16[432,384]{1,0:T(8,128)(2,1)}, u32[]{:S(2)}) %copy-start.2) | copy-done | bytes 331800
  6.6 0.0 copy-start.3
  6.7 0.8 %copy-done.3 = f32[2,5120]{1,0:T(2,128)S(1)} copy-done((f32[2,5120]{1,0:T(2,128)S(1)}, f32[2,5120]{1,0:T(2,128)}, u32[]{:S(2)}) %copy-start.3) | copy-done | bytes 40984
  7.4 0.0 copy-start.4
  7.4 0.7 %copy-done.4 = f32[64]{0:T(128)S(1)} copy-done((f32[64]{0:T(128)S(1)}, f32[64]{0:T(128)}, u32[]{:S(2)}) %copy-start.4) | copy-done | bytes 280
  8.1 0.0 copy-start.5
  8.1 0.7 %copy-done.5 = f32[16]{0:T(128)S(1)} copy-done((f32[16]{0:T(128)S(1)}, f32[16]{0:T(128)}, u32[]{:S(2)}) %copy-start.5) | copy-done | bytes 88
  8.7 0.0 copy-start.6
  8.7 0.7 %copy-done.6 = f32[16]{0:T(128)S(1)} copy-done((f32[16]{0:T(128)S(1)}, f32[16]{0:T(128)}, u32[]{:S(2)}) %copy-start.6) | copy-done | bytes 88
  9.4 25.1 %shard_map.140 = (bf16[4,2,80,384]{3,2,1,0:T(8,128)(2,1)S(1)}, bf16[4,2,80,384]{3,2,1,0:T(8,128)(2,1)S(1)}) custom-call(bf16[160,5120]{1,0:T(8,128)(2,1)} %tok_hbm.1, s32[1]{0:T(128)S(6)} %copy.17.ts_ref, f32[50,5120]{1,0:T(8,128)S(1)} %copy-done, f32[2,5120]{1,0:T(2,128)S(1)} %copy-done.3, bf16[64,5120]{1,0:T(8,128)(2,1)S(1)} %bitcast.5, ...), custom_call_target="tpu_custom_call" | custom-call | tf_op jit(solution)/shard_map/pallas_call | solution.py:368
  34.5 0.8 %copy.18 = bf16[4,2,80,384]{3,2,1,0:T(8,128)(2,1)} copy(bf16[4,2,80,384]{3,2,1,0:T(8,128)(2,1)S(1)} %get-tuple-element.4) | data formatting | bytes 983040
  35.2 0.8 %copy.19 = bf16[4,2,80,384]{3,2,1,0:T(8,128)(2,1)} copy(bf16[4,2,80,384]{3,2,1,0:T(8,128)(2,1)S(1)} %get-tuple-element.5) | data formatting | bytes 983040
Async XLA Ops:
  3.3 1.3 %copy-start = (f32[50,5120]{1,0:T(8,128)S(1)}, f32[50,5120]{1,0:T(8,128)}, u32[]{:S(2)}) copy-start(f32[50,5120]{1,0:T(8,128)} %table_hbm.1) | copy-start | bytes 3072004
  4.6 1.1 %copy-start.1 = (bf16[5120,64]{0,1:T(8,128)(2,1)S(1)}, bf16[5120,64]{0,1:T(8,128)(2,1)}, u32[]{:S(2)}) copy-start(bf16[5120,64]{0,1:T(8,128)(2,1)} %param.17) | copy-start | bytes 1966084
  5.7 1.0 %copy-start.2 = (bf16[432,384]{1,0:T(8,128)(2,1)S(1)}, bf16[432,384]{1,0:T(8,128)(2,1)}, u32[]{:S(2)}) copy-start(bf16[432,384]{1,0:T(8,128)(2,1)} %ciw_ref.1) | copy-start | bytes 995332
  6.6 0.8 %copy-start.3 = (f32[2,5120]{1,0:T(2,128)S(1)}, f32[2,5120]{1,0:T(2,128)}, u32[]{:S(2)}) copy-start(f32[2,5120]{1,0:T(2,128)} %mod_ref.1) | copy-start | bytes 122884
  7.4 0.7 %copy-start.4 = (f32[64]{0:T(128)S(1)}, f32[64]{0:T(128)}, u32[]{:S(2)}) copy-start(f32[64]{0:T(128)} %param.18) | copy-start | bytes 772
  8.1 0.7 %copy-start.5 = (f32[16]{0:T(128)S(1)}, f32[16]{0:T(128)}, u32[]{:S(2)}) copy-start(f32[16]{0:T(128)} %param.19) | copy-start | bytes 196
  8.7 0.7 %copy-start.6 = (f32[16]{0:T(128)S(1)}, f32[16]{0:T(128)}, u32[]{:S(2)}) copy-start(f32[16]{0:T(128)} %param.20) | copy-start | bytes 196

commit v2 on v1

--- a/solution.py
+++ b/solution.py
@@ -24,24 +24,33 @@
     heights,
     widths,
     tok_hbm,
+    ts_hbm,
+    table_hbm,
+    mod_hbm,
+    hw_hbm,
+    hb_hbm,
+    std_hbm,
+    mean_hbm,
+    ciw_hbm,
+    cib_hbm,
+    gain_hbm,
+    w_hbm,
+    cb_hbm,
+    out1,
+    out2,
+    tok,
     ts_ref,
-    table_hbm,
+    table_ref,
     mod_ref,
-    hw_hbm,
+    hw_ref,
     hb_ref,
     std_ref,
     mean_ref,
     ciw_ref,
     cib_ref,
     gain_ref,
-    w_hbm,
+    w_ref,
     cb_ref,
-    out1,
-    out2,
-    tok,
-    table,
-    hw,
-    w,
     modded,
     lat,
     recv,
@@ -59,6 +68,7 @@
     in_sem,
     send_sem,
     recv_sem,
+    fwd_sem,
     peer_sem,
 ):
     ha = lax.axis_index("ha")
@@ -70,23 +80,35 @@
     rows = tok.shape[0]
     cols = rows // 2
     chan = gain_ref.shape[1]
-    half_chan = w.shape[0]
+    half_chan = w_ref.shape[0]
     zch = std_ref.shape[1]
     odd = ha % 2
-
-    table_copy = pltpu.make_async_copy(table_hbm, table, in_sem.at[0])
-    table_copy.start()
 
     def tok_copy(i):
         part = pl.ds(pl.multiple_of(i * CHUNK, CHUNK), CHUNK)
         return pltpu.make_async_copy(tok_hbm.at[part], tok.at[part], tok_sem.at[i])
 
+    ts_copy = pltpu.make_async_copy(ts_hbm, ts_ref, in_sem.at[0])
+    table_copy = pltpu.make_async_copy(table_hbm, table_ref, in_sem.at[1])
+    mod_copy = pltpu.make_async_copy(mod_hbm, mod_ref, in_sem.at[2])
+    hw_copy = pltpu.make_async_copy(hw_hbm, hw_ref, in_sem.at[3])
+    hb_copy = pltpu.make_async_copy(hb_hbm, hb_ref.at[0], in_sem.at[4])
+    std_copy = pltpu.make_async_copy(std_hbm, std_ref.at[0], in_sem.at[5])
+    mean_copy = pltpu.make_async_copy(mean_hbm, mean_ref.at[0], in_sem.at[6])
+    ciw_copy = pltpu.make_async_copy(ciw_hbm, ciw_ref, in_sem.at[7])
+    cib_copy = pltpu.make_async_copy(cib_hbm, cib_ref.at[0], in_sem.at[8])
+    gain_copy = pltpu.make_async_copy(gain_hbm, gain_ref.at[0], in_sem.at[9])
+    cb_copy = pltpu.make_async_copy(cb_hbm, cb_ref.at[0], in_sem.at[10])
+    w_copy = pltpu.make_async_copy(w_hbm, w_ref, in_sem.at[11])
+    ts_copy.start()
+    mod_copy.start()
+    table_copy.start()
     for i in range(rows // CHUNK):
         tok_copy(i).start()
-    hw_copy = pltpu.make_async_copy(hw_hbm, hw, in_sem.at[1])
-    hw_copy.start()
-    w_copy = pltpu.make_async_copy(w_hbm, w, in_sem.at[2])
-    w_copy.start()
+    for copy in (hw_copy, hb_copy, std_copy, mean_copy):
+        copy.start()
+    for copy in (ciw_copy, cib_copy, gain_copy, cb_copy, w_copy):
+        copy.start()
 
     base = ha // 2
 
@@ -97,12 +119,19 @@
             ha + 2 * odd - 1 < heights
         )
 
+    for ff in range(F):
+        for edge, slot in ((0, 0), (heights - 1, 2)):
+
+            @pl.when((ha == edge) & (wa == ff % 2))
+            def _():
+                recv[ff, slot] = jnp.zeros(recv.shape[2:], BF16)
+
     barrier = pltpu.get_barrier_semaphore()
     for ff in range(F):
         for kind in range(2):
             device, exists = source(ff, kind)
 
-            @pl.when(exists & (device != me))
+            @pl.when(exists & (device != me) & (wa == ff % 2))
             def _():
                 pl.semaphore_signal(
                     barrier,
@@ -113,8 +142,10 @@
 
     pl.semaphore_signal(barrier, inc=1, device_id={"wa": 1 - wa}, device_id_type=MESH)
 
+    ts_copy.wait()
+    mod_copy.wait()
     table_copy.wait()
-    embed = table[pl.ds(ts_ref[0], 1), :]
+    embed = table_ref[pl.ds(ts_ref[0], 1), :]
     shift = mod_ref[0:1, :] + embed
     scale = 1.0 + (mod_ref[1:2, :] + embed)
 
@@ -130,39 +161,44 @@
         return carry
 
     lax.fori_loop(0, rows // CHUNK, head_step, 0)
-    hw_copy.wait()
-    projected = dot_t(modded[...], hw[...]) + hb_ref[...]
-    repeats = hw.shape[0] // zch
+    for copy in (hw_copy, hb_copy, std_copy, mean_copy):
+        copy.wait()
+    projected = dot_t(modded[...], hw_ref[...]) + hb_ref[...]
+    repeats = hw_ref.shape[0] // zch
     projected = projected * jnp.concatenate([std_ref[...]] * repeats, axis=1) + jnp.concatenate(
         [mean_ref[...]] * repeats, axis=1
     )
-    lat[...] = (
-        jnp.concatenate([projected, projected], axis=1).astype(BF16).reshape(2, cols, lat.shape[2])
-    )
+    for j in range(2):
+        both = [projected[j * cols + h * PW : j * cols + (h + 1) * PW] for h in range(2)]
+        dense = jnp.concatenate(both, axis=1)
+        filler = jnp.zeros((lat.shape[1] - PW, 128), F32)
+        lat[j] = jnp.concatenate([dense, filler], axis=0).astype(BF16)
 
     plan = ((0, 1, 2, 1), (0, 2, 1, 0), (0, 2, 0, 0), (1, 1, 0, 1))
+
+    to_wa = frame % 2
 
     def targets():
         for k, (row, count, slot, kind) in enumerate(plan):
             to_ha = 2 * pp - 1 + k
-            for to_wa in range(2):
-                valid = (to_ha >= 0) & (to_ha < heights)
-                mine = (to_ha == ha) & (wa == to_wa)
-                copy = pltpu.make_async_remote_copy(
-                    src_ref=lat.at[pl.ds(row, count)],
-                    dst_ref=recv.at[frame, pl.ds(slot, count)],
-                    send_sem=send_sem.at[k, to_wa],
-                    recv_sem=recv_sem.at[frame, kind],
-                    device_id={"ha": to_ha, "wa": to_wa},
-                    device_id_type=MESH,
-                )
-                yield valid, mine, copy, row, count, slot
+            valid = (to_ha >= 0) & (to_ha < heights)
+            mine = (to_ha == ha) & (wa == to_wa)
+            copy = pltpu.make_async_remote_copy(
+                src_ref=lat.at[pl.ds(row, count)],
+                dst_ref=recv.at[frame, pl.ds(slot, count)],
+                send_sem=send_sem.at[k],
+                recv_sem=recv_sem.at[frame, kind],
+                device_id={"ha": to_ha, "wa": to_wa},
+                device_id_type=MESH,
+            )
+            yield valid, mine, copy, row, count, slot
 
     expected = jnp.int32(1)
     for k in range(4):
         to_ha = 2 * pp - 1 + k
         valid = (to_ha >= 0) & (to_ha < heights)
-        expected += jnp.where(valid, 2 - jnp.where(to_ha == ha, 1, 0), 0)
+        mine = (to_ha == ha) & (wa == to_wa)
+        expected += jnp.where(valid & jnp.logical_not(mine), 1, 0)
     pl.semaphore_wait(barrier, expected)
     for valid, mine, copy, row, count, slot in targets():
 
@@ -174,6 +210,8 @@
         def _():
             recv[frame, slot : slot + count] = lat[row : row + count]
 
+    for copy in (ciw_copy, cib_copy, gain_copy, cb_copy):
+        copy.wait()
     wc[...] = jnp.zeros(wc.shape, BF16)
     for a in range(3):
         for win_row in range(4):
@@ -188,14 +226,6 @@
                             c0 = (o_row * 2 + o_col) * chan
                             wc[k0 : k0 + zch, c0 : c0 + chan] = ciw_ref[r0 : r0 + zch, :]
 
-    @pl.when(ha == 0)
-    def _():
-        recv[:, 0] = jnp.zeros((F,) + recv.shape[2:], BF16)
-
-    @pl.when(ha == heights - 1)
-    def _():
-        recv[:, 2] = jnp.zeros((F,) + recv.shape[2:], BF16)
-
     zbuf[...] = jnp.zeros(zbuf.shape, F32)
     lane = lax.broadcasted_iota(jnp.int32, (CP, 128), 1)
     position = lax.broadcasted_iota(jnp.int32, (88, 1), 0)
@@ -203,24 +233,47 @@
     gain = gain_ref[...]
     first = wa == 0
 
+    def forward(ff):
+        return pltpu.make_async_remote_copy(
+            src_ref=recv.at[ff],
+            dst_ref=recv.at[ff],
+            send_sem=fwd_sem.at[0, ff],
+            recv_sem=fwd_sem.at[1, ff],
+            device_id={"wa": 1 - wa},
+            device_id_type=MESH,
+        )
+
     for ff in range(F):
         for kind in range(2):
             device, exists = source(ff, kind)
             slot = (1 - odd) if kind == 0 else 2 * odd
 
-            @pl.when(exists & (device != me))
+            @pl.when(exists & (device != me) & (wa == ff % 2))
             def _():
                 pltpu.make_async_remote_copy(
                     src_ref=lat.at[pl.ds(0, 2 - kind)],
                     dst_ref=recv.at[ff, pl.ds(slot, 2 - kind)],
-                    send_sem=send_sem.at[0, 0],
+                    send_sem=send_sem.at[0],
                     recv_sem=recv_sem.at[ff, kind],
                     device_id={"wa": 1 - wa},
                     device_id_type=MESH,
                 ).wait_recv()
 
+        @pl.when(wa == ff % 2)
+        def _():
+            forward(ff).start()
+
+    for ff in range(F):
+
+        @pl.when(wa != ff % 2)
+        def _():
+            forward(ff).wait_recv()
+
         for t in range(3):
-            zbuf[8 : 8 + cols, :] = recv[ff, t].astype(F32)
+            dense = recv[ff, t].astype(F32)[0:PW]
+            swapped = jnp.concatenate([dense[:, 64:128], dense[:, 0:64]], axis=1)
+            zbuf[8 : 8 + PW, :] = jnp.where(lane[0:PW] < 64, dense, swapped)
+            zbuf[8 + PW : 8 + 2 * PW, :] = jnp.where(lane[0:PW] < 64, swapped, dense)
             left = zbuf[7 : 7 + CP, :]
             right = zbuf[8 : 8 + CP, :]
             pair[ff, t] = jnp.where(lane < 64, left, right).astype(BF16)
@@ -290,6 +343,12 @@
         def _():
             copy.wait_send()
 
+    for ff in range(F):
+
+        @pl.when(wa == ff % 2)
+        def _():
+            forward(ff).wait_send()
+
     w_copy.wait()
     bias = jnp.where(first, cb_ref[:, 0:half_chan], cb_ref[:, half_chan : 2 * half_chan])
     peer_copy = pltpu.make_async_remote_copy(
@@ -311,7 +370,7 @@
             for b in range(3):
                 lhs = act[0:frames, b : b + 2, h].reshape(frames * block, depth)
                 k0 = (3 * a + b) * depth
-                term = dot_t(lhs, w[:, k0 : k0 + depth])
+                term = dot_t(lhs, w_ref[:, k0 : k0 + depth])
                 if a == 2 and b == 0:
                     acc[...] = term
                 else:
@@ -362,36 +421,30 @@
     chan = norm_gain.shape[0]
     half_chan = conv_weight.shape[1]
     whole = pl.BlockSpec(memory_space=pltpu.VMEM)
-    far = pl.BlockSpec(memory_space=pl.ANY)
     out = jax.ShapeDtypeStruct((F, 2, 2 * PW, chan), BF16)
     return tuple(
         pl.pallas_call(
             functools.partial(kernel, heights, widths),
             out_shape=(out, out),
-            in_specs=[
-                far,
-                pl.BlockSpec(memory_space=pltpu.SMEM),
-                far,
-                whole,
-                far,
-                whole,
-                whole,
-                whole,
-                whole,
-                whole,
-                whole,
-                far,
-                whole,
-            ],
+            in_specs=[pl.BlockSpec(memory_space=pltpu.HBM)] * 13,
             out_specs=(whole, whole),
             scratch_shapes=[
                 pltpu.VMEM((rows, width), BF16),
+                pltpu.SMEM((1,), jnp.int32),
                 pltpu.VMEM(time_table.shape, F32),
+                pltpu.VMEM(modulation.shape, F32),
                 pltpu.VMEM(head_weight.shape[::-1], BF16),
+                pltpu.VMEM((1,) + head_bias.shape, F32),
+                pltpu.VMEM((1,) + latent_std.shape, F32),
+                pltpu.VMEM((1,) + latent_mean.shape, F32),
+                pltpu.VMEM(conv_in_weight.shape, BF16),
+                pltpu.VMEM((1, chan), F32),
+                pltpu.VMEM((1, chan), F32),
                 pltpu.VMEM(conv_weight.shape[::-1], BF16),
+                pltpu.VMEM((1, chan), F32),
                 pltpu.VMEM((rows, width), BF16),
-                pltpu.VMEM((2, cols, 128), BF16),
-                pltpu.VMEM((F, 3, cols, 128), BF16),
+                pltpu.VMEM((2, 48, 128), BF16),
+                pltpu.VMEM((F, 3, 48, 128), BF16),
                 pltpu.VMEM((CP + 16, 128), F32),
                 pltpu.VMEM((F, 3, CP, 128), BF16),
                 pltpu.VMEM((768, 4 * chan), BF16),
@@ -403,13 +456,14 @@
                 pltpu.VMEM((F, 2, 2 * PW, half_chan), BF16),
                 pltpu.VMEM((chan // 128, 2 * PW, 128), F32),
                 pltpu.SemaphoreType.DMA((rows // CHUNK,)),
-                pltpu.SemaphoreType.DMA((3,)),
-                pltpu.SemaphoreType.DMA((4, 2)),
+                pltpu.SemaphoreType.DMA((12,)),
+                pltpu.SemaphoreType.DMA((4,)),
                 pltpu.SemaphoreType.DMA((F, 2)),
+                pltpu.SemaphoreType.DMA((2, F)),
                 pltpu.SemaphoreType.DMA((2,)),
             ],
             compiler_params=pltpu.CompilerParams(
-                collective_id=0, has_side_effects=True, vmem_limit_bytes=50 << 20
+                collective_id=0, has_side_effects=True, vmem_limit_bytes=64 << 20
             ),
         )(
             tokens,
@@ -417,14 +471,14 @@
             time_table,
             modulation,
             head_weight.T,
-            head_bias[None],
-            latent_std[None],
-            latent_mean[None],
+            head_bias,
+            latent_std,
+            latent_mean,
             conv_in_weight,
-            conv_in_bias[None],
-            norm_gain[None],
+            conv_in_bias,
+            norm_gain,
             conv_weight.T,
-            conv_bias[None],
+            conv_bias,
         )
     )
 

time: 36.4 us -> 28.4 us (0.78)
  the two profiles are of different devices: /device:TPU:25 before, /device:TPU:0 now
where the time goes in v2:
time: 28.4 us; the launch traced here: 28.2 us
  Pallas kernels  23.2 us (82%)
  local copies, waits for them, and re-layouts  3.71 us (13%)
  between operations  1.29 us (5%)
    pallas_call x1, Pallas kernels, shards(): pl.pallas_call(functools.partial(kernel, heights, widths), out_shape=(out...  23.2 us
    unnamed x2, local copies, waits for them, and re-layouts  3.71 us

profile of v2, /device:TPU:0, one launch (start us, length us, event | category | flops | bytes accessed | tf_op | source)
XLA Modules:
  0.0 28.2 jit_solution(16618530124501716827)
XLA Ops:
  1.3 23.2 %shard_map.140 = (bf16[4,2,80,384]{3,2,1,0:T(8,128)(2,1)}, bf16[4,2,80,384]{3,2,1,0:T(8,128)(2,1)}) custom-call(bf16[160,5120]{1,0:T(8,128)(2,1)} %tok_hbm.1, s32[1]{0:T(128)S(6)} %copy.17.ts_hbm, f32[50,5120]{1,0:T(8,128)} %table_hbm.1, f32[2,5120]{1,0:T(2,128)} %mod_hbm.1, bf16[64,5120]{1,0:T(8,128)(2,1)} %bitcast.3, f32[64]{0:T(128)} %hb_hbm.1, ...), custom_call_target="tpu_custom_call" | custom-call | tf_op jit(solution)/shard_map/pallas_call | solution.py:426
  24.5 1.9 %copy.18 = bf16[4,2,80,384]{3,2,1,0:T(8,128)(2,1)} copy(bf16[4,2,80,384]{3,2,1,0:T(8,128)(2,1)} %get-tuple-element.4) | data formatting | bytes 983040
  26.4 1.9 %copy.19 = bf16[4,2,80,384]{3,2,1,0:T(8,128)(2,1)} copy(bf16[4,2,80,384]{3,2,1,0:T(8,128)(2,1)} %get-tuple-element.5) | data formatting | bytes 983040

commit v3 on v2

--- a/solution.py
+++ b/solution.py
@@ -399,6 +399,18 @@
                 out2[ff, row, :, part] = stage[q].astype(BF16)
 
 
+def deliver(in1, in2, out1, out2, sem):
+    copies = [
+        pltpu.make_async_copy(src.at[ff], dst.at[ff], sem.at[i, ff])
+        for i, (src, dst) in enumerate(((in1, out1), (in2, out2)))
+        for ff in range(F)
+    ]
+    for copy in copies:
+        copy.start()
+    for copy in copies:
+        copy.wait()
+
+
 def shards(
     tokens,
     timestep,
@@ -422,7 +434,7 @@
     half_chan = conv_weight.shape[1]
     whole = pl.BlockSpec(memory_space=pltpu.VMEM)
     out = jax.ShapeDtypeStruct((F, 2, 2 * PW, chan), BF16)
-    return tuple(
+    results = tuple(
         pl.pallas_call(
             functools.partial(kernel, heights, widths),
             out_shape=(out, out),
@@ -481,6 +493,16 @@
             conv_bias,
         )
     )
+    far = pl.BlockSpec(memory_space=pltpu.HBM)
+    return tuple(
+        pl.pallas_call(
+            deliver,
+            out_shape=(out, out),
+            in_specs=[far, far],
+            out_specs=(far, far),
+            scratch_shapes=[pltpu.SemaphoreType.DMA((2, F))],
+        )(*results)
+    )
 
 
 def solution(mesh):

time: 28.4 us -> 55.6 us (1.96)
  Pallas kernels: 23.2 us -> 54.2 us
  local copies, waits for them, and re-layouts: 3.71 us -> 0 us
    pallas_call x0 -> x1, Pallas kernels: none -> 31 us  [shards(): pl.pallas_call(deliver, out_shape=(out, out), in_specs=[far, far], out_sp...]
    unnamed x2 -> x0, local copies, waits for them, and re-layouts: 3.71 us -> none
where the time goes in v3:
time: 55.6 us; the launch traced here: 55.5 us
  Pallas kernels  54.2 us (97%)
  between operations  1.29 us (2%)
    pallas_call x1, Pallas kernels, shards(): pl.pallas_call(deliver, out_shape=(out, out), in_specs=[far, far], out_sp...  31 us
    pallas_call x1, Pallas kernels, shards(): pl.pallas_call(functools.partial(kernel, heights, widths), out_shape=(out...  23.2 us

profile of v3, /device:TPU:0, one launch (start us, length us, event | category | flops | bytes accessed | tf_op | source)
XLA Modules:
  0.0 55.5 jit_solution(7671164056893087643)
XLA Ops:
  1.3 23.2 %shard_map.140 = (bf16[4,2,80,384]{3,2,1,0:T(8,128)(2,1)}, bf16[4,2,80,384]{3,2,1,0:T(8,128)(2,1)}) custom-call(bf16[160,5120]{1,0:T(8,128)(2,1)} %tok_hbm.1, s32[1]{0:T(128)S(6)} %copy.15.ts_hbm, f32[50,5120]{1,0:T(8,128)} %table_hbm.1, f32[2,5120]{1,0:T(2,128)} %mod_hbm.1, bf16[64,5120]{1,0:T(8,128)(2,1)} %bitcast.3, f32[64]{0:T(128)} %hb_hbm.1, ...), custom_call_target="tpu_custom_call" | custom-call | tf_op jit(solution)/shard_map/pallas_call | solution.py:438
  24.5 31.0 %shard_map.141 = (bf16[4,2,80,384]{3,2,1,0:T(8,128)(2,1)}, bf16[4,2,80,384]{3,2,1,0:T(8,128)(2,1)}) custom-call(bf16[4,2,80,384]{3,2,1,0:T(8,128)(2,1)} %get-tuple-element.4.in1, bf16[4,2,80,384]{3,2,1,0:T(8,128)(2,1)} %get-tuple-element.5.in2), custom_call_target="tpu_custom_call" | custom-call | tf_op jit(solution)/shard_map/pallas_call | solution.py:498
